TPU v7x, 32 devices: a whole 2x2x4 slice. The times are simulated.
32 devices in a mesh: seq: 8 (over y, x, core), head: 4 (over z).
Axes of the slice: x: 2, y: 2, z: 4, core: 2. Of those that a mesh axis runs over, the one named last changes fastest.
Arguments:
- projected: bfloat16 [4096, 3, 3072], P(('seq', 'head')), may hold values from -70 to 70
- key_lists: int32 [48, 32, 8], P('head', 'seq'), may hold values from 0 to 31, as said below
- list_counts: int32 [48, 32], P('head', 'seq'), may hold values from 1 to 8
Outputs:
- attended: bfloat16 [4096, 3072], P(('seq', 'head'))
Inputs may be any that keep to these rules, and one draw needn't show every extreme that they name: `key_lists`: entries are key block numbers; no list names its own query block, and the entries of one list are distinct. Entry j of the list of query block b in head h lies on seq shard (b // 4 + o + j) mod 8, o depending on h and b. Over the 12 heads of one head group and the query blocks of one seq shard, exactly 48 entries lie on each seq shard, entries past a list's count included, and the entries that lie on one seq shard name at most two distinct key blocks: at most one whose number within its shard is below 2 and at most one whose number is at least that. In every draw some head group, seq shard and owning seq shard have two.
All inputs are finite; a program needn't handle non-finite values.
Results may differ from a plain program's by a relative error of at most 0.005.
Values may be sent and summed in bfloat16 or wider, within the bound.
No kernel may reach another device: no remote copies, remote signals or barrier semaphores. Data moves between devices by JAX's collectives and lax.ppermute only.
A program may use at most 128 MiB of HBM per device.

v0:
```python
import math
import jax
import jax.numpy as jnp
from jax import lax
from jax.sharding import PartitionSpec as P

NEG_FILL = -1e30


def attend_rows(query_part, gathered, live_cols, head_size):
    row_count, seen_blocks, block_len, doubled = gathered.shape
    key_rows = gathered[..., :head_size].reshape(row_count, seen_blocks * block_len, head_size)
    value_rows = gathered[..., head_size:].reshape(row_count, seen_blocks * block_len, head_size)
    attention_scores = jnp.einsum(
        "rqd,rkd->rqk", query_part, key_rows, preferred_element_type=jnp.float32
    ) * (1.0 / math.sqrt(head_size))
    attention_scores = attention_scores.reshape(row_count, block_len, seen_blocks, block_len)
    attention_scores = jnp.where(live_cols[:, None, :, None], attention_scores, NEG_FILL)
    row_top = jnp.max(attention_scores, axis=(2, 3), keepdims=True)
    exp_scores = jnp.exp(attention_scores - row_top)
    attention_weights = (exp_scores / jnp.sum(exp_scores, axis=(2, 3), keepdims=True)).astype(
        jnp.bfloat16
    )
    attention_weights = attention_weights.reshape(row_count, block_len, seen_blocks * block_len)
    return jnp.einsum(
        "rqk,rkd->rqd", attention_weights, value_rows, preferred_element_type=jnp.float32
    )


def on_device(projected, key_lists, list_counts):
    seq_count = lax.axis_size("seq")
    heads_dev, blocks_dev, list_most = key_lists.shape
    regrouped = lax.all_to_all(projected, "head", split_axis=2, concat_axis=0, tiled=True)
    block_len = regrouped.shape[0] // blocks_dev
    group_width = regrouped.shape[2]
    head_size = group_width // heads_dev
    row_count = heads_dev * blocks_dev
    splitted = regrouped.reshape(blocks_dev, block_len, 3, heads_dev, head_size)
    queries = splitted[:, :, 0].transpose(2, 0, 1, 3).reshape(row_count, block_len, head_size)
    kv_pairs = jnp.concatenate([splitted[:, :, 1], splitted[:, :, 2]], axis=-1)
    kv_pairs = kv_pairs.transpose(2, 0, 1, 3).reshape(row_count, block_len, 2 * head_size)
    entries = key_lists.reshape(row_count * list_most)
    owners = entries // blocks_dev
    row_head = jnp.arange(row_count * list_most, dtype=jnp.int32) // (blocks_dev * list_most)
    capacity = row_count * list_most // seq_count
    wanted = row_head * blocks_dev + entries % blocks_dev
    onehot = (owners[:, None] == jnp.arange(seq_count, dtype=jnp.int32)[None, :]).astype(jnp.int32)
    within = jnp.sum(onehot * (jnp.cumsum(onehot, axis=0) - 1), axis=1)
    slot_ids = owners * capacity + within
    request = (
        jnp.zeros((seq_count * capacity,), jnp.int32)
        .at[slot_ids]
        .set(wanted)
        .reshape(seq_count, capacity)
    )
    asked_for = lax.all_to_all(request, "seq", split_axis=0, concat_axis=0, tiled=True)
    served = jnp.take(kv_pairs, asked_for.reshape(-1), axis=0).reshape(
        seq_count, capacity, block_len, 2 * head_size
    )
    fetched = lax.all_to_all(served, "seq", split_axis=0, concat_axis=0, tiled=True)
    fetched = fetched.reshape(seq_count * capacity, block_len, 2 * head_size)
    entry_slots = slot_ids.reshape(row_count, list_most)
    row_counts = list_counts.reshape(row_count)
    group_rows = 4

    def one_group(group_index):
        start = group_index * group_rows
        query_part = lax.dynamic_slice_in_dim(queries, start, group_rows, 0)
        own_pairs = lax.dynamic_slice_in_dim(kv_pairs, start, group_rows, 0)
        slot_part = lax.dynamic_slice_in_dim(entry_slots, start, group_rows, 0)
        count_part = lax.dynamic_slice_in_dim(row_counts, start, group_rows, 0)
        listed = jnp.take(fetched, slot_part.reshape(-1), axis=0).reshape(
            group_rows, list_most, block_len, 2 * head_size
        )
        gathered = jnp.concatenate([own_pairs[:, None], listed], axis=1)
        live_cols = jnp.concatenate(
            [
                jnp.ones((group_rows, 1), bool),
                jnp.arange(list_most, dtype=jnp.int32)[None, :] < count_part[:, None],
            ],
            axis=1,
        )
        return attend_rows(query_part, gathered, live_cols, head_size).astype(jnp.bfloat16)

    attended = lax.map(one_group, jnp.arange(row_count // group_rows, dtype=jnp.int32))
    attended = attended.reshape(row_count, block_len, head_size)
    laid_out = attended.reshape(heads_dev, blocks_dev * block_len, head_size).transpose(1, 0, 2)
    laid_out = laid_out.reshape(blocks_dev * block_len, group_width)
    return lax.all_to_all(laid_out, "head", split_axis=0, concat_axis=1, tiled=True)


def solution(mesh):
    return jax.shard_map(
        on_device,
        mesh=mesh,
        in_specs=(P(("seq", "head"), None, None), P("head", "seq", None), P("head", "seq")),
        out_specs=P(("seq", "head"), None),
        check_vma=False,
    )
```

profile of v0, /device:TPU:2, one launch (start us, length us, event | category | flops | bytes accessed | tf_op | source)
XLA Modules:
  0.0 542.2 jit_solution(7548757384802746488)
XLA Ops:
  2.4 2.9 scatter_custom_fusion
  6.0 4.3 all-to-all-start.1
  10.3 5.7 %copy.35 = bf16[128,3,3072]{0,1,2:T(4,128)(2,1)} copy(bf16[128,3,3072]{2,0,1:T(8,128)(2,1)} %param.5) | data formatting | bytes 4718592 | tf_op args[0]
  16.0 4.9 all-to-all-start
  22.1 69.7 %all-to-all-done = bf16[128,3,3072]{0,1,2:T(4,128)(2,1)S(1)} async-done(((bf16[128,3,3072]{0,1,2:T(4,128)(2,1)}), bf16[128,3,3072]{0,1,2:T(4,128)(2,1)S(1)}, u32[]{:S(2)}, u32[]{:S(2)}) %all-to-all-start) | async-done | bytes 2359328 | tf_op jit(solution)/shard_map/all_to_all | solution.py:33
  94.5 11.3 %gather_fusion.1 = bf16[384,128,128]{2,1,0:T(8,128)(2,1)} fusion(bf16[48,128,128]{2,1,0:T(8,128)(2,1)S(1)} %bitcast.78, s32[1024]{0:T(1024)S(1)} %pad_clamp_fusion.1), kind=kCustom, calls=%fused_computation.1 | custom fusion | bytes 25167360 | tf_op jit(solution)/shard_map/jit(_take)/gather | solution.py:57
  105.8 10.8 %broadcast_select_fusion.1 = bf16[8,48,128,128]{3,2,1,0:T(8,128)(2,1)} fusion(bf16[8,48,128,128]{3,2,1,0:T(8,128)(2,1)} %bitcast.81, pred[8,48]{1,0:T(8,128)(4,1)S(1)} %compare_and_fusion.1), kind=kLoop, calls=%fused_computation.39 | loop fusion | flops 6291456 | bytes 25166208 | tf_op jit(solution)/shard_map/jit(_take)/select_n | solution.py:57
  116.6 5.7 %all-to-all-start.2 = ((bf16[8,48,128,128]{3,2,1,0:T(8,128)(2,1)}), bf16[8,48,128,128]{3,2,1,0:T(8,128)(2,1)}, u32[]{:S(2)}, u32[]{:S(2)}) async-start(bf16[8,48,128,128]{3,2,1,0:T(8,128)(2,1)} %broadcast_select_fusion.1), calls=%async_computation.2 | async-start | bytes 25165824 | tf_op jit(solution)/shard_map/all_to_all | solution.py:60
  123.6 136.3 %all-to-all-done.2 = bf16[8,48,128,128]{3,2,1,0:T(8,128)(2,1)} async-done(((bf16[8,48,128,128]{3,2,1,0:T(8,128)(2,1)}), bf16[8,48,128,128]{3,2,1,0:T(8,128)(2,1)}, u32[]{:S(2)}, u32[]{:S(2)}) %all-to-all-start.2) | async-done | bytes 12582944 | tf_op jit(solution)/shard_map/all_to_all | solution.py:60
  259.9 256.2 %while.10 = (s32[]{:T(128)}, bf16[12,4,128,64]{2,1,3,0:T(4,128)(2,1)}, s32[12]{0:T(128)S(1)}, s32[48]{0:T(128)S(1)}, bf16[48,128,64]{1,2,0:T(8,128)(2,1)}, /*ind...) while((s32[]{:T(128)}, ...), condition=%wide.region_7.8_spmd, body=%wide.region_4.7_spmd.sunk | while | flops 234721344 | bytes 13664708 | solution.py:85
  261.2 6.3 %gather_fusion = bf16[32,128,128]{2,1,0:T(8,128)(2,1)} fusion(bf16[384,128,128]{2,1,0:T(8,128)(2,1)} %get-tuple-element.162, s32[1024]{0:T(1024)S(1)} %pad_clamp_fusion.3), kind=kCustom, calls=%fused_computation.clone.1 | custom fusion | bytes 2097280 | tf_op jit(solution)/shard_map/while/body/eval_jaxpr/jit(_take)/gather | solution.py:72
  267.6 1.7 copy.62
  270.6 3.0 fusion.71
  275.4 1.8 fusion.72
  278.4 2.2 fusion.73
  282.6 6.3 %gather_fusion = bf16[32,128,128]{2,1,0:T(8,128)(2,1)} fusion(bf16[384,128,128]{2,1,0:T(8,128)(2,1)} %get-tuple-element.162, s32[1024]{0:T(1024)S(1)} %pad_clamp_fusion.3), kind=kCustom, calls=%fused_computation.clone.1 | custom fusion | bytes 2097280 | tf_op jit(solution)/shard_map/while/body/eval_jaxpr/jit(_take)/gather | solution.py:72
  288.9 1.7 copy.62
  292.0 3.0 fusion.71
  296.8 1.8 fusion.72
  299.7 2.2 fusion.73
  303.9 6.3 %gather_fusion = bf16[32,128,128]{2,1,0:T(8,128)(2,1)} fusion(bf16[384,128,128]{2,1,0:T(8,128)(2,1)} %get-tuple-element.162, s32[1024]{0:T(1024)S(1)} %pad_clamp_fusion.3), kind=kCustom, calls=%fused_computation.clone.1 | custom fusion | bytes 2097280 | tf_op jit(solution)/shard_map/while/body/eval_jaxpr/jit(_take)/gather | solution.py:72
  310.2 1.7 copy.62
  313.3 3.0 fusion.71
  318.1 1.8 fusion.72
  321.1 2.2 fusion.73
  325.3 6.3 %gather_fusion = bf16[32,128,128]{2,1,0:T(8,128)(2,1)} fusion(bf16[384,128,128]{2,1,0:T(8,128)(2,1)} %get-tuple-element.162, s32[1024]{0:T(1024)S(1)} %pad_clamp_fusion.3), kind=kCustom, calls=%fused_computation.clone.1 | custom fusion | bytes 2097280 | tf_op jit(solution)/shard_map/while/body/eval_jaxpr/jit(_take)/gather | solution.py:72
  334.7 3.0 fusion.71
  339.5 1.8 fusion.72
  342.4 2.2 fusion.73
  346.6 6.3 %gather_fusion = bf16[32,128,128]{2,1,0:T(8,128)(2,1)} fusion(bf16[384,128,128]{2,1,0:T(8,128)(2,1)} %get-tuple-element.162, s32[1024]{0:T(1024)S(1)} %pad_clamp_fusion.3), kind=kCustom, calls=%fused_computation.clone.1 | custom fusion | bytes 2097280 | tf_op jit(solution)/shard_map/while/body/eval_jaxpr/jit(_take)/gather | solution.py:72
  352.9 1.7 copy.62
  356.0 3.0 fusion.71
  360.8 1.8 fusion.72
  363.8 2.2 fusion.73
  368.0 6.3 %gather_fusion = bf16[32,128,128]{2,1,0:T(8,128)(2,1)} fusion(bf16[384,128,128]{2,1,0:T(8,128)(2,1)} %get-tuple-element.162, s32[1024]{0:T(1024)S(1)} %pad_clamp_fusion.3), kind=kCustom, calls=%fused_computation.clone.1 | custom fusion | bytes 2097280 | tf_op jit(solution)/shard_map/while/body/eval_jaxpr/jit(_take)/gather | solution.py:72
  374.3 1.7 copy.62
  377.4 3.0 fusion.71
  382.2 1.8 fusion.72
  385.1 2.2 fusion.73
  389.3 6.3 %gather_fusion = bf16[32,128,128]{2,1,0:T(8,128)(2,1)} fusion(bf16[384,128,128]{2,1,0:T(8,128)(2,1)} %get-tuple-element.162, s32[1024]{0:T(1024)S(1)} %pad_clamp_fusion.3), kind=kCustom, calls=%fused_computation.clone.1 | custom fusion | bytes 2097280 | tf_op jit(solution)/shard_map/while/body/eval_jaxpr/jit(_take)/gather | solution.py:72
  398.7 3.0 fusion.71
  403.5 1.8 fusion.72
  406.4 2.2 fusion.73
  410.7 6.3 %gather_fusion = bf16[32,128,128]{2,1,0:T(8,128)(2,1)} fusion(bf16[384,128,128]{2,1,0:T(8,128)(2,1)} %get-tuple-element.162, s32[1024]{0:T(1024)S(1)} %pad_clamp_fusion.3), kind=kCustom, calls=%fused_computation.clone.1 | custom fusion | bytes 2097280 | tf_op jit(solution)/shard_map/while/body/eval_jaxpr/jit(_take)/gather | solution.py:72
  420.1 3.0 fusion.71
  424.9 1.8 fusion.72
  427.8 2.2 fusion.73
  432.0 6.3 %gather_fusion = bf16[32,128,128]{2,1,0:T(8,128)(2,1)} fusion(bf16[384,128,128]{2,1,0:T(8,128)(2,1)} %get-tuple-element.162, s32[1024]{0:T(1024)S(1)} %pad_clamp_fusion.3), kind=kCustom, calls=%fused_computation.clone.1 | custom fusion | bytes 2097280 | tf_op jit(solution)/shard_map/while/body/eval_jaxpr/jit(_take)/gather | solution.py:72
  441.4 3.0 fusion.71
  446.2 1.8 fusion.72
  449.1 2.2 fusion.73
  453.4 6.3 %gather_fusion = bf16[32,128,128]{2,1,0:T(8,128)(2,1)} fusion(bf16[384,128,128]{2,1,0:T(8,128)(2,1)} %get-tuple-element.162, s32[1024]{0:T(1024)S(1)} %pad_clamp_fusion.3), kind=kCustom, calls=%fused_computation.clone.1 | custom fusion | bytes 2097280 | tf_op jit(solution)/shard_map/while/body/eval_jaxpr/jit(_take)/gather | solution.py:72
  462.8 3.0 fusion.71
  467.5 1.8 fusion.72
  470.5 2.2 fusion.73
  474.7 6.3 %gather_fusion = bf16[32,128,128]{2,1,0:T(8,128)(2,1)} fusion(bf16[384,128,128]{2,1,0:T(8,128)(2,1)} %get-tuple-element.162, s32[1024]{0:T(1024)S(1)} %pad_clamp_fusion.3), kind=kCustom, calls=%fused_computation.clone.1 | custom fusion | bytes 2097280 | tf_op jit(solution)/shard_map/while/body/eval_jaxpr/jit(_take)/gather | solution.py:72
  484.1 3.0 fusion.71
  488.9 1.8 fusion.72
  491.8 2.2 fusion.73
  496.1 6.3 %gather_fusion = bf16[32,128,128]{2,1,0:T(8,128)(2,1)} fusion(bf16[384,128,128]{2,1,0:T(8,128)(2,1)} %get-tuple-element.162, s32[1024]{0:T(1024)S(1)} %pad_clamp_fusion.3), kind=kCustom, calls=%fused_computation.clone.1 | custom fusion | bytes 2097280 | tf_op jit(solution)/shard_map/while/body/eval_jaxpr/jit(_take)/gather | solution.py:72
  505.5 3.0 fusion.71
  510.2 1.8 fusion.72
  513.2 2.2 fusion.73
  518.0 23.0 %all_to_all.48 = bf16[4,128,768]{1,2,0:T(8,128)(2,1)S(1)} all-to-all(bf16[4,128,768]{1,2,0:T(8,128)(2,1)S(1)} %copy.46), channel_id=1, replica_groups=mesh['seq'=8,'head'=4] {'head'}, dimensions={0} | all-to-all | bytes 1572864 | tf_op jit(solution)/shard_map/all_to_all | solution.py:89
  (240 shorter events, 92.3 us)
Async XLA Ops:
  6.0 9.9 %all-to-all-start.1 = ((s32[8,1,48]{2,1,0:T(1,128)}), s32[8,1,48]{2,1,0:T(1,128)S(1)}, u32[]{:S(2)}, u32[]{:S(2)}) async-start(s32[8,1,48]{2,1,0:T(1,128)} %all_to_all.37), calls=%async_computation.1 | async-start | bytes 8192 | tf_op jit(solution)/shard_map/all_to_all | solution.py:56
  16.0 75.9 %all-to-all-start = ((bf16[128,3,3072]{0,1,2:T(4,128)(2,1)}), bf16[128,3,3072]{0,1,2:T(4,128)(2,1)S(1)}, u32[]{:S(2)}, u32[]{:S(2)}) async-start(bf16[128,3,3072]{0,1,2:T(4,128)(2,1)} %copy.35), calls=%async_computation | async-start | bytes 6291456 | tf_op jit(solution)/shard_map/all_to_all | solution.py:33
  116.6 5.8 %copy-start.1 = (s32[12,4]{0,1:T(4,128)S(1)}, s32[12,4]{0,1:T(4,128)}, u32[]{:S(2)}) copy-start(s32[12,4]{0,1:T(4,128)} %param.7) | copy-start | bytes 580
  116.6 6.0 %copy-start = (bf16[12,4,128,64]{2,3,0,1:T(8,128)(2,1)S(1)}, bf16[12,4,128,64]{2,3,0,1:T(8,128)(2,1)}, u32[]{:S(2)}) copy-start(bf16[12,4,128,64]{2,3,0,1:T(8,128)(2,1)} %get-tuple-element.69) | copy-start | bytes 2359300
  116.6 143.3 %all-to-all-start.2 = ((bf16[8,48,128,128]{3,2,1,0:T(8,128)(2,1)}), bf16[8,48,128,128]{3,2,1,0:T(8,128)(2,1)}, u32[]{:S(2)}, u32[]{:S(2)}) async-start(bf16[8,48,128,128]{3,2,1,0:T(8,128)(2,1)} %broadcast_select_fusion.1), calls=%async_computation.2 | async-start | bytes 25165824 | tf_op jit(solution)/shard_map/all_to_all | solution.py:60
where the time goes:
time: 545 us; the launch traced here: 542 us
  waiting for transfers between devices  206 us (38%)
  local copies, waits for them, and re-layouts  178 us (33%)
  other arithmetic  64.3 us (12%)
  matrix products  47.5 us (9%)
  blocking collectives  23 us (4%)
  starting transfers between devices  14.8 us (3%)
  loops' own time  8.01 us (1%)
    all_to_all x1, waiting for transfers between devices, on_device(): lax.all_to_all(served, 'seq', split_axis=0, concat_axis=0, tiled=True)  136 us
    gather x24, local copies, waits for them, and re-layouts, one_group(): jnp.take(fetched, slot_part.reshape(-1), axis=0)  95.7 us
    all_to_all x1, waiting for transfers between devices, on_device(): lax.all_to_all(projected, 'head', split_axis=2, concat_axis=0, tiled=True)  69.7 us
    concatenate x12, other arithmetic, one_group(): gathered = jnp.concatenate([own_pairs[:, None], listed], axis=1)  35.8 us
    dot_general x12, matrix products, attend_rows(): jnp.einsum('rqk,rkd->rqd', attention_weights, value_rows, preferred_eleme...  26.2 us
    all_to_all x1, blocking collectives, on_device(): lax.all_to_all(laid_out, 'head', split_axis=0, concat_axis=1, tiled=True)  23 us
    sub x12, matrix products, attend_rows(): exp_scores = jnp.exp(attention_scores - row_top)  21.2 us
    reshape x12, local copies, waits for them, and re-layouts, attend_rows(): gathered[..., :head_size]  17.7 us
  transfers between devices with their start and end apart: 3, of which 2 were waited for; matrix products, arithmetic and copies ran while one was open for 2% of the time, Pallas kernels for 0%

commit v1 on v0

--- a/solution.py
+++ b/solution.py
@@ -1,3 +1,4 @@
+import functools
 import math
 import jax
 import jax.numpy as jnp
@@ -5,6 +6,36 @@
 from jax.sharding import PartitionSpec as P
 
 NEG_FILL = -1e30
+
+
+def solve_quarters_over_axis(local_array, on_dim, buf):
+    reached = local_array.shape
+    tile_out = local_array.reshape(
+        *reached[:on_dim], buf, reached[on_dim] // buf, *reached[on_dim + 1 :]
+    )
+    return jnp.moveaxis(tile_out, on_dim, 0)
+
+
+def pools_fill(local, d0):
+    local = jnp.moveaxis(local, 0, d0)
+    mat_out = local.shape
+    return local.reshape(*mat_out[:d0], mat_out[d0] * mat_out[d0 + 1], *mat_out[d0 + 2 :])
+
+
+def return_all_the_words(work_x, comm_axis, z_in, local_x):
+    t1, then = (jax.lax.axis_size(comm_axis), jax.lax.axis_index(comm_axis))
+    k_now = solve_quarters_over_axis(work_x, z_in, t1)
+    all_rows = [k_now[then]]
+    for k0 in tuple(range(1, t1)):
+        r1 = k_now[then ^ k0]
+        all_rows.append(
+            jax.lax.ppermute(r1, axis_name=comm_axis, perm=[(b, b ^ k0) for b in range(t1)])
+        )
+    k_now = jnp.stack(all_rows)[then ^ jnp.arange(t1)]
+    return pools_fill(k_now, local_x)
+
+
+target_put = functools.partial(return_all_the_words, comm_axis="seq", z_in=0, local_x=0)
 
 
 def attend_rows(query_part, gathered, live_cols, head_size):
@@ -57,7 +88,7 @@
     served = jnp.take(kv_pairs, asked_for.reshape(-1), axis=0).reshape(
         seq_count, capacity, block_len, 2 * head_size
     )
-    fetched = lax.all_to_all(served, "seq", split_axis=0, concat_axis=0, tiled=True)
+    fetched = target_put(served)
     fetched = fetched.reshape(seq_count * capacity, block_len, 2 * head_size)
     entry_slots = slot_ids.reshape(row_count, list_most)
     row_counts = list_counts.reshape(row_count)

time: 545 us -> 563 us (1.033)
  local copies, waits for them, and re-layouts: 178 us -> 214 us
  waiting for transfers between devices: 206 us -> 192 us
    all_to_all x1 -> x0, waiting for transfers between devices: 136 us -> none  [on_device(): lax.all_to_all(served, 'seq', split_axis=0, concat_axis=0, tiled=True)]
    ppermute x0 -> x7, waiting for transfers between devices: none -> 122 us  [return_all_the_words(): jax.lax.ppermute(r1, axis_name=comm_axis, perm=[(b, b ^ k0) for b in rang...]
    unnamed x7 -> x13, local copies, waits for them, and re-layouts: 6.61 us -> 23.1 us
    gather x0 -> x1, local copies, waits for them, and re-layouts: none -> 11 us  [return_all_the_words(): k_now = jnp.stack(all_rows)[then ^ jnp.arange(t1)]]
    all_to_all x1 -> x0, starting transfers between devices: 5.72 us -> none  [on_device(): lax.all_to_all(served, 'seq', split_axis=0, concat_axis=0, tiled=True)]
  transfers between devices with their start and end apart: 3 -> 9, of which waited for: 2 -> 5; matrix products, arithmetic and copies ran while one was open for 2% -> 4% of each run, Pallas kernels for 0% -> 0%
where the time goes in v1:
time: 563 us; the launch traced here: 559 us
  local copies, waits for them, and re-layouts  214 us (38%)
  waiting for transfers between devices  192 us (34%)
  other arithmetic  60 us (11%)
  matrix products  47.5 us (8%)
  blocking collectives  23.4 us (4%)
  starting transfers between devices  14.4 us (3%)
  loops' own time  8.01 us (1%)
    ppermute x7, waiting for transfers between devices, return_all_the_words(): jax.lax.ppermute(r1, axis_name=comm_axis, perm=[(b, b ^ k0) for b in rang...  122 us
    gather x24, local copies, waits for them, and re-layouts, one_group(): jnp.take(fetched, slot_part.reshape(-1), axis=0)  95.7 us
    all_to_all x1, waiting for transfers between devices, on_device(): lax.all_to_all(projected, 'head', split_axis=2, concat_axis=0, tiled=True)  69.9 us
    concatenate x12, other arithmetic, one_group(): gathered = jnp.concatenate([own_pairs[:, None], listed], axis=1)  35.8 us
    dot_general x12, matrix products, attend_rows(): jnp.einsum('rqk,rkd->rqd', attention_weights, value_rows, preferred_eleme...  26.2 us
    all_to_all x1, blocking collectives, on_device(): lax.all_to_all(laid_out, 'head', split_axis=0, concat_axis=1, tiled=True)  23.4 us
    unnamed x13, local copies, waits for them, and re-layouts  23.1 us
    sub x12, matrix products, attend_rows(): exp_scores = jnp.exp(attention_scores - row_top)  21.2 us
  transfers between devices with their start and end apart: 9, of which 5 were waited for; matrix products, arithmetic and copies ran while one was open for 4% of the time, Pallas kernels for 0%

profile of v1, /device:TPU:2, one launch (start us, length us, event | category | flops | bytes accessed | tf_op | source)
XLA Modules:
  0.0 559.0 jit_solution(9776444709007312853)
XLA Ops:
  2.4 2.9 scatter_custom_fusion
  6.0 4.3 all-to-all-start.1
  10.3 5.7 %copy.34 = bf16[128,3,3072]{0,1,2:T(4,128)(2,1)} copy(bf16[128,3,3072]{2,0,1:T(8,128)(2,1)} %param.5) | data formatting | bytes 4718592 | tf_op args[0]
  15.9 4.9 all-to-all-start
  22.1 69.9 %all-to-all-done = bf16[128,3,3072]{0,1,2:T(4,128)(2,1)} async-done(((bf16[128,3,3072]{0,1,2:T(4,128)(2,1)}), bf16[128,3,3072]{0,1,2:T(4,128)(2,1)}, u32[]{:S(2)}, u32[]{:S(2)}) %all-to-all-start) | async-done | bytes 2359328 | tf_op jit(solution)/shard_map/all_to_all | solution.py:64
  92.0 2.2 copy.35
  96.6 11.3 %gather_fusion.1 = bf16[384,128,128]{2,1,0:T(8,128)(2,1)} fusion(bf16[48,128,128]{2,1,0:T(8,128)(2,1)S(1)} %bitcast.109, s32[1024]{0:T(1024)S(1)} %pad_clamp_fusion.2), kind=kCustom, calls=%fused_computation.1 | custom fusion | bytes 25167360 | tf_op jit(solution)/shard_map/jit(_take)/gather | solution.py:88
  107.9 6.5 %broadcast_select_fusion.1 = bf16[8,1,48,128,128]{4,3,2,0,1:T(8,128)(2,1)S(1)} fusion(bf16[8,1,48,128,128]{4,3,2,0,1:T(8,128)(2,1)} %bitcast.112, pred[8,48]{1,0:T(8,128)(4,1)S(1)} %compare_and_fusion.1), kind=kLoop, calls=%fused_computation.40 | loop fusion | flops 6291456 | bytes 25166208 | tf_op jit(solution)/shard_map/jit(_take)/select_n | solution.py:88
  114.4 4.7 dynamic-slice_bitcast_fusion.1
  125.5 31.2 %collective-permute-done.1 = bf16[1,48,128,128]{3,2,1,0:T(8,128)(2,1)} collective-permute-done((bf16[1,48,128,128]{3,2,1,0:T(8,128)(2,1)}, bf16[1,48,128,128]{3,2,1,0:T(8,128)(2,1)}, u32[]{:S(2)}, u32[]{:S(2)}) %collective-permute-start.1) | collective-permute-done | bytes 1572896 | tf_op jit(solution)/shard_map/ppermute | solution.py:32
  157.0 2.7 bitcast_dynamic-update-slice_fusion.6
  159.7 2.7 bitcast_dynamic-update-slice_fusion.5
  162.4 27.1 %collective-permute-done.2 = bf16[1,48,128,128]{3,2,1,0:T(8,128)(2,1)} collective-permute-done((bf16[1,48,128,128]{3,2,1,0:T(8,128)(2,1)}, bf16[1,48,128,128]{3,2,1,0:T(8,128)(2,1)}, u32[]{:S(2)}, u32[]{:S(2)}) %collective-permute-start.2) | collective-permute-done | bytes 1572896 | tf_op jit(solution)/shard_map/ppermute | solution.py:32
  189.5 2.8 bitcast_dynamic-update-slice_fusion.4
  192.3 2.7 bitcast_dynamic-update-slice_fusion.3
  195.0 63.5 %collective-permute-done.4 = bf16[1,48,128,128]{3,2,1,0:T(8,128)(2,1)} collective-permute-done((bf16[1,48,128,128]{3,2,1,0:T(8,128)(2,1)}, bf16[1,48,128,128]{3,2,1,0:T(8,128)(2,1)}, u32[]{:S(2)}, u32[]{:S(2)}) %collective-permute-start.4) | collective-permute-done | bytes 1572896 | tf_op jit(solution)/shard_map/ppermute | solution.py:32
  258.5 2.8 bitcast_dynamic-update-slice_fusion.2
  261.3 2.8 bitcast_dynamic-update-slice_fusion.1
  265.3 11.0 %gather_fusion.2 = bf16[8,48,128,128]{3,2,1,0:T(8,128)(2,1)} fusion(bf16[8,48,128,128]{3,2,1,0:T(8,128)(2,1)} %bitcast.114, s32[1024]{0:T(1024)S(1)} %pad_clamp_fusion.1), kind=kCustom, calls=%fused_computation.2 | custom fusion | bytes 25165856 | tf_op jit(solution)/shard_map/gather | solution.py:34
  276.3 256.2 %while.10 = (s32[]{:T(128)}, bf16[12,4,128,64]{2,1,3,0:T(4,128)(2,1)}, s32[12]{0:T(128)S(1)}, s32[48]{0:T(128)S(1)}, bf16[48,128,64]{1,2,0:T(8,128)(2,1)}, /*ind...) while((s32[]{:T(128)}, ...), condition=%wide.region_7.8_spmd, body=%wide.region_4.7_spmd.sunk | while | flops 234721344 | bytes 13664708 | solution.py:116
  277.7 6.3 %gather_fusion = bf16[32,128,128]{2,1,0:T(8,128)(2,1)} fusion(bf16[384,128,128]{2,1,0:T(8,128)(2,1)} %get-tuple-element.170, s32[1024]{0:T(1024)S(1)} %pad_clamp_fusion.4), kind=kCustom, calls=%fused_computation.clone.1 | custom fusion | bytes 2097280 | tf_op jit(solution)/shard_map/while/body/eval_jaxpr/jit(_take)/gather | solution.py:103
  287.1 3.0 fusion.72
  291.8 1.8 fusion.73
  294.8 2.2 fusion.74
  299.0 6.3 %gather_fusion = bf16[32,128,128]{2,1,0:T(8,128)(2,1)} fusion(bf16[384,128,128]{2,1,0:T(8,128)(2,1)} %get-tuple-element.170, s32[1024]{0:T(1024)S(1)} %pad_clamp_fusion.4), kind=kCustom, calls=%fused_computation.clone.1 | custom fusion | bytes 2097280 | tf_op jit(solution)/shard_map/while/body/eval_jaxpr/jit(_take)/gather | solution.py:103
  308.4 3.0 fusion.72
  313.2 1.8 fusion.73
  316.1 2.2 fusion.74
  320.4 6.3 %gather_fusion = bf16[32,128,128]{2,1,0:T(8,128)(2,1)} fusion(bf16[384,128,128]{2,1,0:T(8,128)(2,1)} %get-tuple-element.170, s32[1024]{0:T(1024)S(1)} %pad_clamp_fusion.4), kind=kCustom, calls=%fused_computation.clone.1 | custom fusion | bytes 2097280 | tf_op jit(solution)/shard_map/while/body/eval_jaxpr/jit(_take)/gather | solution.py:103
  329.7 3.0 fusion.72
  334.5 1.8 fusion.73
  337.5 2.2 fusion.74
  341.7 6.3 %gather_fusion = bf16[32,128,128]{2,1,0:T(8,128)(2,1)} fusion(bf16[384,128,128]{2,1,0:T(8,128)(2,1)} %get-tuple-element.170, s32[1024]{0:T(1024)S(1)} %pad_clamp_fusion.4), kind=kCustom, calls=%fused_computation.clone.1 | custom fusion | bytes 2097280 | tf_op jit(solution)/shard_map/while/body/eval_jaxpr/jit(_take)/gather | solution.py:103
  351.1 3.0 fusion.72
  355.9 1.8 fusion.73
  358.8 2.2 fusion.74
  363.1 6.3 %gather_fusion = bf16[32,128,128]{2,1,0:T(8,128)(2,1)} fusion(bf16[384,128,128]{2,1,0:T(8,128)(2,1)} %get-tuple-element.170, s32[1024]{0:T(1024)S(1)} %pad_clamp_fusion.4), kind=kCustom, calls=%fused_computation.clone.1 | custom fusion | bytes 2097280 | tf_op jit(solution)/shard_map/while/body/eval_jaxpr/jit(_take)/gather | solution.py:103
  372.4 3.0 fusion.72
  377.2 1.8 fusion.73
  380.2 2.2 fusion.74
  384.4 6.3 %gather_fusion = bf16[32,128,128]{2,1,0:T(8,128)(2,1)} fusion(bf16[384,128,128]{2,1,0:T(8,128)(2,1)} %get-tuple-element.170, s32[1024]{0:T(1024)S(1)} %pad_clamp_fusion.4), kind=kCustom, calls=%fused_computation.clone.1 | custom fusion | bytes 2097280 | tf_op jit(solution)/shard_map/while/body/eval_jaxpr/jit(_take)/gather | solution.py:103
  393.8 3.0 fusion.72
  398.6 1.8 fusion.73
  401.5 2.2 fusion.74
  405.8 6.3 %gather_fusion = bf16[32,128,128]{2,1,0:T(8,128)(2,1)} fusion(bf16[384,128,128]{2,1,0:T(8,128)(2,1)} %get-tuple-element.170, s32[1024]{0:T(1024)S(1)} %pad_clamp_fusion.4), kind=kCustom, calls=%fused_computation.clone.1 | custom fusion | bytes 2097280 | tf_op jit(solution)/shard_map/while/body/eval_jaxpr/jit(_take)/gather | solution.py:103
  415.1 3.0 fusion.72
  419.9 1.8 fusion.73
  422.9 2.2 fusion.74
  427.1 6.3 %gather_fusion = bf16[32,128,128]{2,1,0:T(8,128)(2,1)} fusion(bf16[384,128,128]{2,1,0:T(8,128)(2,1)} %get-tuple-element.170, s32[1024]{0:T(1024)S(1)} %pad_clamp_fusion.4), kind=kCustom, calls=%fused_computation.clone.1 | custom fusion | bytes 2097280 | tf_op jit(solution)/shard_map/while/body/eval_jaxpr/jit(_take)/gather | solution.py:103
  436.5 3.0 fusion.72
  444.2 2.2 fusion.74
  448.4 6.3 %gather_fusion = bf16[32,128,128]{2,1,0:T(8,128)(2,1)} fusion(bf16[384,128,128]{2,1,0:T(8,128)(2,1)} %get-tuple-element.170, s32[1024]{0:T(1024)S(1)} %pad_clamp_fusion.4), kind=kCustom, calls=%fused_computation.clone.1 | custom fusion | bytes 2097280 | tf_op jit(solution)/shard_map/while/body/eval_jaxpr/jit(_take)/gather | solution.py:103
  457.8 3.0 fusion.72
  465.6 2.2 fusion.74
  469.8 6.3 %gather_fusion = bf16[32,128,128]{2,1,0:T(8,128)(2,1)} fusion(bf16[384,128,128]{2,1,0:T(8,128)(2,1)} %get-tuple-element.170, s32[1024]{0:T(1024)S(1)} %pad_clamp_fusion.4), kind=kCustom, calls=%fused_computation.clone.1 | custom fusion | bytes 2097280 | tf_op jit(solution)/shard_map/while/body/eval_jaxpr/jit(_take)/gather | solution.py:103
  479.2 3.0 fusion.72
  486.9 2.2 fusion.74
  491.1 6.3 %gather_fusion = bf16[32,128,128]{2,1,0:T(8,128)(2,1)} fusion(bf16[384,128,128]{2,1,0:T(8,128)(2,1)} %get-tuple-element.170, s32[1024]{0:T(1024)S(1)} %pad_clamp_fusion.4), kind=kCustom, calls=%fused_computation.clone.1 | custom fusion | bytes 2097280 | tf_op jit(solution)/shard_map/while/body/eval_jaxpr/jit(_take)/gather | solution.py:103
  500.5 3.0 fusion.72
  508.3 2.2 fusion.74
  512.5 6.3 %gather_fusion = bf16[32,128,128]{2,1,0:T(8,128)(2,1)} fusion(bf16[384,128,128]{2,1,0:T(8,128)(2,1)} %get-tuple-element.170, s32[1024]{0:T(1024)S(1)} %pad_clamp_fusion.4), kind=kCustom, calls=%fused_computation.clone.1 | custom fusion | bytes 2097280 | tf_op jit(solution)/shard_map/while/body/eval_jaxpr/jit(_take)/gather | solution.py:103
  521.9 3.0 fusion.72
  529.6 2.2 fusion.74
  534.4 23.4 %all_to_all.43 = bf16[4,128,768]{1,2,0:T(8,128)(2,1)S(1)} all-to-all(bf16[4,128,768]{1,2,0:T(8,128)(2,1)S(1)} %copy.45), channel_id=1, replica_groups=mesh['seq'=8,'head'=4] {'head'}, dimensions={0} | all-to-all | bytes 1572864 | tf_op jit(solution)/shard_map/all_to_all | solution.py:120
  (263 shorter events, 115.7 us)
Async XLA Ops:
  6.0 9.9 %all-to-all-start.1 = ((s32[8,1,48]{2,1,0:T(1,128)}), s32[8,1,48]{2,1,0:T(1,128)S(1)}, u32[]{:S(2)}, u32[]{:S(2)}) async-start(s32[8,1,48]{2,1,0:T(1,128)} %all_to_all.34), calls=%async_computation.1 | async-start | bytes 8192 | tf_op jit(solution)/shard_map/all_to_all | solution.py:87
  15.9 76.1 %all-to-all-start = ((bf16[128,3,3072]{0,1,2:T(4,128)(2,1)}), bf16[128,3,3072]{0,1,2:T(4,128)(2,1)}, u32[]{:S(2)}, u32[]{:S(2)}) async-start(bf16[128,3,3072]{0,1,2:T(4,128)(2,1)} %copy.34), calls=%async_computation | async-start | bytes 6291456 | tf_op jit(solution)/shard_map/all_to_all | solution.py:64
  114.4 10.0 %copy-start.1 = (s32[12,4]{0,1:T(4,128)S(1)}, s32[12,4]{0,1:T(4,128)}, u32[]{:S(2)}) copy-start(s32[12,4]{0,1:T(4,128)} %param.7) | copy-start | bytes 580
  114.4 10.1 %copy-start = (bf16[12,4,128,64]{2,3,0,1:T(8,128)(2,1)S(1)}, bf16[12,4,128,64]{2,3,0,1:T(8,128)(2,1)}, u32[]{:S(2)}) copy-start(bf16[12,4,128,64]{2,3,0,1:T(8,128)(2,1)} %get-tuple-element.77) | copy-start | bytes 2359300
  119.1 3.8 collective-permute-start
  119.1 37.6 %collective-permute-start.1 = (bf16[1,48,128,128]{3,2,1,0:T(8,128)(2,1)}, bf16[1,48,128,128]{3,2,1,0:T(8,128)(2,1)}, u32[]{:S(2)}, u32[]{:S(2)}) collective-permute-start(bf16[1,48,128,128]{3,2,1,0:T(8,128)(2,1)} %get-tuple-element.73), channel_id=1, source_target_pairs={{0,8},{4,12},{8,0},{12,4},{16,24},{20,28},{24,16},{28,20},{1,9},{5... | collective-permute-start | bytes 4718600 | tf_op jit(solution)/shard_map/ppermute | solution.py:32
  119.6 70.0 %collective-permute-start.2 = (bf16[1,48,128,128]{3,2,1,0:T(8,128)(2,1)}, bf16[1,48,128,128]{3,2,1,0:T(8,128)(2,1)}, u32[]{:S(2)}, u32[]{:S(2)}) collective-permute-start(bf16[1,48,128,128]{3,2,1,0:T(8,128)(2,1)} %get-tuple-element.72), channel_id=1, source_target_pairs={{0,12},{4,8},{8,4},{12,0},{16,28},{20,24},{24,20},{28,16},{1,13},{... | collective-permute-start | bytes 4718600 | tf_op jit(solution)/shard_map/ppermute | solution.py:32
  121.0 71.3 %collective-permute-start.3 = (bf16[1,48,128,128]{3,2,1,0:T(8,128)(2,1)}, bf16[1,48,128,128]{3,2,1,0:T(8,128)(2,1)}, u32[]{:S(2)}, u32[]{:S(2)}) collective-permute-start(bf16[1,48,128,128]{3,2,1,0:T(8,128)(2,1)} %get-tuple-element.71), channel_id=1, source_target_pairs={{0,16},{4,20},{8,24},{12,28},{16,0},{20,4},{24,8},{28,12},{1,17},{... | collective-permute-start | bytes 4718600 | tf_op jit(solution)/shard_map/ppermute | solution.py:32
  122.5 136.0 %collective-permute-start.4 = (bf16[1,48,128,128]{3,2,1,0:T(8,128)(2,1)}, bf16[1,48,128,128]{3,2,1,0:T(8,128)(2,1)}, u32[]{:S(2)}, u32[]{:S(2)}) collective-permute-start(bf16[1,48,128,128]{3,2,1,0:T(8,128)(2,1)} %get-tuple-element.70), channel_id=1, source_target_pairs={{0,20},{4,16},{8,28},{12,24},{16,4},{20,0},{24,12},{28,8},{1,21},{... | collective-permute-start | bytes 4718600 | tf_op jit(solution)/shard_map/ppermute | solution.py:32
  122.9 138.4 %collective-permute-start.5 = (bf16[1,48,128,128]{3,2,1,0:T(8,128)(2,1)}, bf16[1,48,128,128]{3,2,1,0:T(8,128)(2,1)}, u32[]{:S(2)}, u32[]{:S(2)}) collective-permute-start(bf16[1,48,128,128]{3,2,1,0:T(8,128)(2,1)} %get-tuple-element.69), channel_id=1, source_target_pairs={{0,24},{4,28},{8,16},{12,20},{16,8},{20,12},{24,0},{28,4},{1,25},{... | collective-permute-start | bytes 4718600 | tf_op jit(solution)/shard_map/ppermute | solution.py:32
  156.7 107.3 %collective-permute-start.6 = (bf16[1,48,128,128]{3,2,1,0:T(8,128)(2,1)}, bf16[1,48,128,128]{3,2,1,0:T(8,128)(2,1)S(1)}, u32[]{:S(2)}, u32[]{:S(2)}) collective-permute-start(bf16[1,48,128,128]{3,2,1,0:T(8,128)(2,1)} %get-tuple-element.68), channel_id=1, source_target_pairs={{0,28},{4,24},{8,20},{12,16},{16,12},{20,8},{24,4},{28,0},{1,29},{... | collective-permute-start | bytes 4718600 | tf_op jit(solution)/shard_map/ppermute | solution.py:32
